TPU v7x, 32 devices: a whole 2x2x4 slice. The times are simulated.
32 devices in a mesh: ctx: 16 (over z, x, core), chan: 2 (over y).
Axes of the slice: x: 2, y: 2, z: 4, core: 2. Of those that a mesh axis runs over, the one named last changes fastest.
Arguments:
- query_act: bfloat16 [2048, 1024], P('ctx', 'chan'), may hold values from -6 to 6
- key_act: bfloat16 [2048, 1024], P('ctx', 'chan'), may hold values from -6 to 6
- value_act: bfloat16 [2048, 1024], P('ctx', 'chan'), may hold values from -6 to 6
- filters: bfloat16 [2048, 1024], P('ctx', 'chan'), may hold values from -0.125 to 0.125
- skip_scale: float32 [1024], P('chan'), may hold values from -4 to 4
- w_out: bfloat16 [1024, 4096], P('chan'), may hold values from -0.25 to 0.25
Outputs:
- projected: bfloat16 [2048, 4096], P('ctx', 'chan')
All inputs are finite; a program needn't handle non-finite values.
Results may differ from a plain program's by a relative error of at most 0.015.
Values may be sent and summed in bfloat16 or wider, within the bound.
A program may use at most 64 MiB of HBM per device.

v0:
```python
import math
import jax
import jax.numpy as jnp
from jax import lax
from jax.sharding import PartitionSpec as P

precise = lax.Precision.HIGHEST


def phase_table(row_count, col_count, modulus, factor):
    row_index = lax.broadcasted_iota(jnp.int32, (row_count, col_count), 0)
    col_index = lax.broadcasted_iota(jnp.int32, (row_count, col_count), 1)
    phase_angle = (row_index * col_index % modulus).astype(jnp.float32) * (2.0 * math.pi / modulus)
    return (jnp.cos(phase_angle) * factor, jnp.sin(phase_angle) * factor)


def twiddle(freq_index, pos_index, modulus):
    phase_angle = (freq_index * pos_index % modulus).astype(jnp.float32) * (2.0 * math.pi / modulus)
    return (jnp.cos(phase_angle), jnp.sin(phase_angle))


def shards(query_act, key_act, value_act, filters, skip_scale, w_out):
    tok_rows, chan_width = key_act.shape
    ctx_size = lax.axis_size("ctx")
    per_dev = tok_rows // ctx_size
    fft_length = 2 * tok_rows * ctx_size
    freq_blocks = 2 * ctx_size
    ctx_index = lax.axis_index("ctx")
    gated_in = (key_act.astype(jnp.float32) * value_act.astype(jnp.float32)).astype(jnp.bfloat16)
    sent_input, sent_filter = (
        lax.all_to_all(
            gated_in.reshape(1, ctx_size, per_dev, chan_width),
            "ctx",
            split_axis=1,
            concat_axis=0,
            tiled=True,
        ),
        lax.all_to_all(
            filters.reshape(1, ctx_size, per_dev, chan_width),
            "ctx",
            split_axis=1,
            concat_axis=0,
            tiled=True,
        ),
    )
    block_cos, block_sin = phase_table(freq_blocks, ctx_size, freq_blocks, 1.0)
    offsets = ctx_index * per_dev + lax.broadcasted_iota(jnp.int32, (1, per_dev), 1)
    all_freq = lax.broadcasted_iota(jnp.int32, (freq_blocks, 1), 0)
    front_cos, front_sin = twiddle(all_freq, offsets, fft_length)
    front_cos = front_cos[:, :, None]
    front_sin = front_sin[:, :, None]

    def first_section(signal):
        values32 = signal.reshape(ctx_size, per_dev, chan_width).astype(jnp.float32)
        real_part = jnp.einsum("kp,pjc->kjc", block_cos, values32, precision=precise)
        imag_part = -jnp.einsum("kp,pjc->kjc", block_sin, values32, precision=precise)
        out_real = real_part * front_cos + imag_part * front_sin
        out_imag = imag_part * front_cos - real_part * front_sin
        return jnp.stack([out_real, out_imag]).reshape(2, ctx_size, 2, per_dev, chan_width)

    cycle_cos, cycle_sin = phase_table(tok_rows, tok_rows, tok_rows, 1.0)

    def cycle_apply(table, operand):
        return jnp.einsum("kn,zmnc->zmkc", table, operand, precision=precise)

    spec_input = lax.all_to_all(
        first_section(sent_input), "ctx", split_axis=1, concat_axis=3, tiled=True
    )
    spec_filter = lax.all_to_all(
        first_section(sent_filter), "ctx", split_axis=1, concat_axis=3, tiled=True
    )

    def forward(portion):
        real_in = portion[0]
        imag_in = portion[1]
        out_real = cycle_apply(cycle_cos, real_in) + cycle_apply(cycle_sin, imag_in)
        out_imag = cycle_apply(cycle_cos, imag_in) - cycle_apply(cycle_sin, real_in)
        return (out_real, out_imag)

    input_real, input_imag = forward(spec_input)
    filter_real, filter_imag = forward(spec_filter)
    prod_real = input_real * filter_real - input_imag * filter_imag
    prod_imag = input_real * filter_imag + input_imag * filter_real
    back_real = cycle_apply(cycle_cos, prod_real) - cycle_apply(cycle_sin, prod_imag)
    back_imag = cycle_apply(cycle_cos, prod_imag) + cycle_apply(cycle_sin, prod_real)
    mixed = jnp.stack([back_real, back_imag])
    inverted = mixed[:, 0]
    pack_width = inverted.shape[-1]
    own_freq = 2 * ctx_index + lax.broadcasted_iota(jnp.int32, (2, 1), 0)
    all_offsets = lax.broadcasted_iota(jnp.int32, (1, tok_rows), 1)
    back_cos, back_sin = twiddle(own_freq, all_offsets, fft_length)
    back_cos = back_cos[:, :, None]
    back_sin = back_sin[:, :, None]
    turned_real = inverted[0] * back_cos - inverted[1] * back_sin
    turned_imag = inverted[0] * back_sin + inverted[1] * back_cos
    turned = jnp.stack([turned_real, turned_imag]).reshape(2, 2, ctx_size, per_dev, pack_width)
    last_cos, last_sin = phase_table(ctx_size, freq_blocks, freq_blocks, 1.0 / fft_length)

    def last_apply(table, operand):
        return jnp.einsum("nk,kzmc->nzmc", table, operand, precision=precise)

    portion = lax.all_to_all(turned, "ctx", split_axis=2, concat_axis=1, tiled=True)
    returned = last_apply(last_cos, portion[0]) - last_apply(last_sin, portion[1])
    convolved = lax.all_to_all(returned, "ctx", split_axis=0, concat_axis=1, tiled=True).reshape(
        tok_rows, chan_width
    )
    gated = (
        query_act.astype(jnp.float32)
        * (convolved + skip_scale[None, :] * gated_in.astype(jnp.float32))
    ).astype(jnp.bfloat16)
    summed = lax.psum_scatter(
        lax.dot_general(
            w_out, gated, (((0,), (1,)), ((), ())), preferred_element_type=jnp.float32
        ).astype(jnp.bfloat16),
        "chan",
        scatter_dimension=0,
        tiled=True,
    )
    return summed.T


def solution(mesh):
    return jax.shard_map(
        shards,
        mesh=mesh,
        in_specs=(
            P("ctx", "chan"),
            P("ctx", "chan"),
            P("ctx", "chan"),
            P("ctx", "chan"),
            P("chan"),
            P("chan", None),
        ),
        out_specs=P("ctx", "chan"),
        check_vma=False,
    )
```

profile of v0, /device:TPU:0, one launch (start us, length us, event | category | flops | bytes accessed | tf_op | source)
XLA Modules:
  0.0 180.7 jit_solution(6431051070737040364)
XLA Ops:
  6.5 1.7 fusion.49
  8.2 7.4 %all-to-all-start = ((bf16[1,16,8,512]{3,2,0,1:T(8,128)(2,1)}), bf16[1,16,8,512]{3,2,0,1:T(8,128)(2,1)S(1)}, u32[]{:S(2)}, u32[]{:S(2)}) async-start(bf16[1,16,8,512]{3,2,0,1:T(8,128)(2,1)} %fusion.49), calls=%async_computation | async-start | bytes 262144 | tf_op jit(solution)/shard_map/all_to_all | solution.py:31
  15.6 0.1 fusion.103
  15.7 7.8 %all-to-all-done = bf16[1,16,8,512]{3,2,0,1:T(8,128)(2,1)S(1)} async-done(((bf16[1,16,8,512]{3,2,0,1:T(8,128)(2,1)}), bf16[1,16,8,512]{3,2,0,1:T(8,128)(2,1)S(1)}, u32[]{:S(2)}, u32[]{:S(2)}) %all-to-all-start) | async-done | bytes 131104 | tf_op jit(solution)/shard_map/all_to_all | solution.py:31
  23.5 3.5 %all-to-all-start.2 = ((bf16[1,16,8,512]{3,2,0,1:T(8,128)(2,1)}), bf16[1,16,8,512]{3,2,0,1:T(8,128)(2,1)S(1)}, u32[]{:S(2)}, u32[]{:S(2)}) async-start(bf16[1,16,8,512]{3,2,0,1:T(8,128)(2,1)} %bitcast.166), calls=%async_computation.2 | async-start | bytes 262144 | tf_op jit(solution)/shard_map/all_to_all | solution.py:38
  27.0 0.5 convolution_negate_fusion.1
  27.5 0.5 fusion.24
  28.0 6.9 %all-to-all-done.2 = bf16[1,16,8,512]{3,2,0,1:T(8,128)(2,1)S(1)} async-done(((bf16[1,16,8,512]{3,2,0,1:T(8,128)(2,1)}), bf16[1,16,8,512]{3,2,0,1:T(8,128)(2,1)S(1)}, u32[]{:S(2)}, u32[]{:S(2)}) %all-to-all-start.2) | async-done | bytes 131104 | tf_op jit(solution)/shard_map/all_to_all | solution.py:38
  34.9 0.5 fusion.21
  35.4 0.6 multiply_add_fusion.1
  36.0 0.3 copy.79
  36.4 0.3 copy.80
  36.7 1.1 pad_maximum_fusion.1
  37.8 3.7 %all-to-all-start.3 = ((f32[2,16,2,8,512]{4,3,2,0,1:T(8,128)}), f32[2,16,2,8,512]{4,3,2,0,1:T(8,128)S(1)}, u32[]{:S(2)}, u32[]{:S(2)}) async-start(f32[2,16,2,8,512]{4,3,2,0,1:T(8,128)} %pad_maximum_fusion.1), calls=%async_computation.3 | async-start | bytes 2097152 | tf_op jit(solution)/shard_map/all_to_all | solution.py:69
  41.4 0.3 copy.78
  41.7 0.3 copy.77
  42.1 1.1 pad_maximum_fusion
  43.1 21.2 %all-to-all-done.3 = f32[2,16,2,8,512]{4,3,2,0,1:T(8,128)S(1)} async-done(((f32[2,16,2,8,512]{4,3,2,0,1:T(8,128)}), f32[2,16,2,8,512]{4,3,2,0,1:T(8,128)S(1)}, u32[]{:S(2)}, u32[]{:S(2)}) %all-to-all-start.3) | async-done | bytes 1048608 | tf_op jit(solution)/shard_map/all_to_all | solution.py:69
  64.3 6.8 %all-to-all-start.1 = ((f32[2,16,2,8,512]{4,3,2,0,1:T(8,128)}), f32[2,16,2,8,512]{4,3,2,0,1:T(8,128)S(1)}, u32[]{:S(2)}, u32[]{:S(2)}) async-start(f32[2,16,2,8,512]{4,3,2,0,1:T(8,128)} %pad_maximum_fusion), calls=%async_computation.1 | async-start | bytes 2097152 | tf_op jit(solution)/shard_map/all_to_all | solution.py:66
  71.1 0.2 reduce-scatter.2.cloned.1.call-start
  71.4 0.1 fusion.108
  71.5 0.1 copy.108
  71.6 1.1 fusion.16
  72.7 1.1 fusion.15
  73.8 20.2 %all-to-all-done.1 = f32[2,16,2,8,512]{4,3,2,0,1:T(8,128)S(1)} async-done(((f32[2,16,2,8,512]{4,3,2,0,1:T(8,128)}), f32[2,16,2,8,512]{4,3,2,0,1:T(8,128)S(1)}, u32[]{:S(2)}, u32[]{:S(2)}) %all-to-all-start.1) | async-done | bytes 1048608 | tf_op jit(solution)/shard_map/all_to_all | solution.py:66
  94.1 0.1 copy.109
  94.2 1.1 fusion.14
  95.3 1.1 fusion.13
  96.4 1.1 convolution_subtract_fusion.1
  97.5 1.1 convolution_add_fusion.1
  98.7 1.1 convolution_add_fusion.2
  99.8 1.1 multiply_subtract_fusion
  100.9 0.9 fusion.8
  101.8 0.9 fusion.10
  102.7 0.9 fusion.1
  103.6 1.2 subtract_bitcast_fusion
  104.8 0.1 pad_maximum_fusion.2
  104.9 0.0 copy-start.1
  105.0 0.1 copy.81
  105.1 31.8 %all_to_all.72 = f32[2,2,16,8,512]{4,3,1,0,2:T(8,128)S(1)} all-to-all(f32[2,2,16,8,512]{4,3,1,0,2:T(8,128)S(1)} %copy.81), channel_id=1, replica_groups=mesh['ctx'=16,'chan'=2] {'ctx'}, dimensions={2} | all-to-all | bytes 2097152 | tf_op jit(solution)/shard_map/all_to_all | solution.py:102
  136.8 0.1 fusion.183
  136.9 0.7 fusion.5
  137.6 0.7 fusion.3
  138.3 0.2 copy.64
  138.5 14.8 %all_to_all.73 = f32[16,1,8,512]{3,2,1,0:T(8,128)S(1)} all-to-all(f32[16,1,8,512]{3,2,1,0:T(8,128)S(1)} %copy.64), channel_id=1, replica_groups=mesh['ctx'=16,'chan'=2] {'ctx'}, dimensions={0} | all-to-all | bytes 524288 | tf_op jit(solution)/shard_map/all_to_all | solution.py:104
  153.3 1.7 fusion
  155.0 0.0 reduce-scatter.2.cloned.1.call-update
  155.1 18.8 %reduce-scatter.2.cloned.1.call-done = bf16[2048,128]{0,1:T(8,128)(2,1)} async-done(((bf16[4096,128]{0,1:T(8,128)(2,1)}), bf16[2048,128]{0,1:T(8,128)(2,1)}) %reduce-scatter.2.cloned.1.call-update) | async-done | bytes 524304 | tf_op jit(solution)/shard_map/reduce_scatter | solution.py:111
  (11 shorter events, 0.0 us)
Async XLA Ops:
  8.2 15.3 %all-to-all-start = ((bf16[1,16,8,512]{3,2,0,1:T(8,128)(2,1)}), bf16[1,16,8,512]{3,2,0,1:T(8,128)(2,1)S(1)}, u32[]{:S(2)}, u32[]{:S(2)}) async-start(bf16[1,16,8,512]{3,2,0,1:T(8,128)(2,1)} %fusion.49), calls=%async_computation | async-start | bytes 262144 | tf_op jit(solution)/shard_map/all_to_all | solution.py:31
  23.5 11.4 %all-to-all-start.2 = ((bf16[1,16,8,512]{3,2,0,1:T(8,128)(2,1)}), bf16[1,16,8,512]{3,2,0,1:T(8,128)(2,1)S(1)}, u32[]{:S(2)}, u32[]{:S(2)}) async-start(bf16[1,16,8,512]{3,2,0,1:T(8,128)(2,1)} %bitcast.166), calls=%async_computation.2 | async-start | bytes 262144 | tf_op jit(solution)/shard_map/all_to_all | solution.py:38
  37.8 26.6 %all-to-all-start.3 = ((f32[2,16,2,8,512]{4,3,2,0,1:T(8,128)}), f32[2,16,2,8,512]{4,3,2,0,1:T(8,128)S(1)}, u32[]{:S(2)}, u32[]{:S(2)}) async-start(f32[2,16,2,8,512]{4,3,2,0,1:T(8,128)} %pad_maximum_fusion.1), calls=%async_computation.3 | async-start | bytes 2097152 | tf_op jit(solution)/shard_map/all_to_all | solution.py:69
  64.3 29.8 %all-to-all-start.1 = ((f32[2,16,2,8,512]{4,3,2,0,1:T(8,128)}), f32[2,16,2,8,512]{4,3,2,0,1:T(8,128)S(1)}, u32[]{:S(2)}, u32[]{:S(2)}) async-start(f32[2,16,2,8,512]{4,3,2,0,1:T(8,128)} %pad_maximum_fusion), calls=%async_computation.1 | async-start | bytes 2097152 | tf_op jit(solution)/shard_map/all_to_all | solution.py:66
  71.1 102.7 %reduce-scatter.2.cloned.1.call-start = ((), (), s32[]{:S(2)}) async-start(), calls=%async_computation.7 | async-start | bytes 1572864 | tf_op jit(solution)/shard_map/reduce_scatter | solution.py:111
  104.9 48.4 %copy-start = (bf16[512,4096]{1,0:T(8,128)(2,1)S(1)}, bf16[512,4096]{1,0:T(8,128)(2,1)}, u32[]{:S(2)}) copy-start(bf16[512,4096]{1,0:T(8,128)(2,1)} %param.11) | copy-start | bytes 12582916
  104.9 48.4 %copy-start.1 = (bf16[128,512]{1,0:T(8,128)(2,1)S(1)}, bf16[128,512]{1,0:T(8,128)(2,1)}, u32[]{:S(2)}) copy-start(bf16[128,512]{1,0:T(8,128)(2,1)} %param.8) | copy-start | bytes 393220
  104.9 48.4 %copy-start.2 = (bf16[128,512]{1,0:T(8,128)(2,1)S(1)}, bf16[128,512]{1,0:T(8,128)(2,1)}, u32[]{:S(2)}) copy-start(bf16[128,512]{1,0:T(8,128)(2,1)} %param.7) | copy-start | bytes 393220
  104.9 48.4 %copy-start.3 = (bf16[128,512]{1,0:T(8,128)(2,1)S(1)}, bf16[128,512]{1,0:T(8,128)(2,1)}, u32[]{:S(2)}) copy-start(bf16[128,512]{1,0:T(8,128)(2,1)} %param.6) | copy-start | bytes 393220
  105.0 48.4 %copy-start.4 = (f32[512]{0:T(512)S(1)}, f32[512]{0:T(512)}, u32[]{:S(2)}) copy-start(f32[512]{0:T(512)} %param.10) | copy-start | bytes 6148
Sparse Core Ops, SparseCore 0:
  155.2 18.6 reduce-scatter.1
where the time goes:
time: 181 us
  waiting for transfers between devices  75 us (41%)
  blocking collectives  46.6 us (26%)
  starting transfers between devices  21.6 us (12%)
  matrix products  17.9 us (10%)
  between operations  13.7 us (8%)
  other arithmetic  4.15 us (2%)
    all_to_all x1, blocking collectives, shards(): lax.all_to_all(turned, 'ctx', split_axis=2, concat_axis=1, tiled=True)  31.8 us
    all_to_all x1, waiting for transfers between devices, shards(): lax.all_to_all(first_section(sent_filter), 'ctx', split_axis=1, concat_ax...  21.2 us
    all_to_all x1, waiting for transfers between devices, shards(): lax.all_to_all(first_section(sent_input), 'ctx', split_axis=1, concat_axi...  20.2 us
    reduce_scatter x1, waiting for transfers between devices, shards(): lax.psum_scatter(lax.dot_general(w_out, gated, (((0,), (1,)), ((), ())),...  18.8 us
    all_to_all x1, blocking collectives, shards(): lax.all_to_all(returned, 'ctx', split_axis=0, concat_axis=1, tiled=True)  14.8 us
    dot_general x12, matrix products, cycle_apply(): return jnp.einsum('kn,zmnc->zmkc', table, operand, precision=precise)  12.8 us
    all_to_all x1, waiting for transfers between devices, shards(): lax.all_to_all(gated_in.reshape(1, ctx_size, per_dev, chan_width), 'ctx',...  7.8 us
    all_to_all x1, starting transfers between devices, shards(): lax.all_to_all(gated_in.reshape(1, ctx_size, per_dev, chan_width), 'ctx',...  7.36 us
  transfers between devices with their start and end apart: 5, of which 5 were waited for; matrix products, arithmetic and copies ran while one was open for 3% of the time, Pallas kernels for 0%

commit v1 on v0

--- a/solution.py
+++ b/solution.py
@@ -5,6 +5,29 @@
 from jax.sharding import PartitionSpec as P
 
 precise = lax.Precision.HIGHEST
+
+
+def split_up(x, dim, size):
+    shape = x.shape
+    pieces = x.reshape(*shape[:dim], size, shape[dim] // size, *shape[dim + 1 :])
+    return jnp.moveaxis(pieces, dim, 0)
+
+
+def joined_along(blocks, dim):
+    blocks = jnp.moveaxis(blocks, 0, dim)
+    dims = blocks.shape
+    return blocks.reshape(*dims[:dim], dims[dim] * dims[dim + 1], *dims[dim + 2 :])
+
+
+def pairwise_exchange(value, axis, split_dim, concat_dim):
+    count, mine = (lax.axis_size(axis), lax.axis_index(axis))
+    blocks = split_up(value, split_dim, count)
+    finished = [blocks[mine]]
+    for step in range(1, count):
+        sent = blocks[mine ^ step]
+        finished.append(lax.ppermute(sent, axis, [(i, i ^ step) for i in range(count)]))
+    blocks = jnp.stack(finished)[mine ^ jnp.arange(count)]
+    return joined_along(blocks, concat_dim)
 
 
 def phase_table(row_count, col_count, modulus, factor):
@@ -101,9 +124,7 @@
 
     portion = lax.all_to_all(turned, "ctx", split_axis=2, concat_axis=1, tiled=True)
     returned = last_apply(last_cos, portion[0]) - last_apply(last_sin, portion[1])
-    convolved = lax.all_to_all(returned, "ctx", split_axis=0, concat_axis=1, tiled=True).reshape(
-        tok_rows, chan_width
-    )
+    convolved = pairwise_exchange(returned, "ctx", 0, 1).reshape(tok_rows, chan_width)
     gated = (
         query_act.astype(jnp.float32)
         * (convolved + skip_scale[None, :] * gated_in.astype(jnp.float32))

time: 181 us -> 197 us (1.088)
  blocking collectives: 46.6 us -> 0 us
  starting transfers between devices: 21.6 us -> 51.4 us
  waiting for transfers between devices: 75 us -> 103 us
  matrix products: 17.9 us -> 20.1 us
    all_to_all x2 -> x0, blocking collectives: 46.6 us -> none  [the longest x1 31.8 us: shards(): lax.all_to_all(turned, 'ctx', split_axis=2, concat_axis=1, tiled=True)]
    ppermute x0 -> x15, starting transfers between devices: none -> 22.8 us  [pairwise_exchange(): lax.ppermute(sent, axis, [(i, i ^ step) for i in range(count)])]
    all_to_all x0 -> x1, waiting for transfers between devices: none -> 22.8 us  [shards(): lax.all_to_all(turned, 'ctx', split_axis=2, concat_axis=1, tiled=True)]
    all_to_all x0 -> x1, starting transfers between devices: none -> 7.01 us  [shards(): lax.all_to_all(turned, 'ctx', split_axis=2, concat_axis=1, tiled=True)]
    ppermute x0 -> x15, waiting for transfers between devices: none -> 4.86 us  [pairwise_exchange(): lax.ppermute(sent, axis, [(i, i ^ step) for i in range(count)])]
    dot_general x1, matrix products: 1.7 us -> 3.89 us  [shards(): lax.dot_general(w_out, gated, (((0,), (1,)), ((), ())), preferred_element...]
  transfers between devices with their start and end apart: 5 -> 21, of which waited for: 5 -> 8; matrix products, arithmetic and copies ran while one was open for 3% -> 3% of each run, Pallas kernels for 0% -> 0%
where the time goes in v1:
time: 197 us; the launch traced here: 196 us
  waiting for transfers between devices  103 us (52%)
  starting transfers between devices  51.4 us (26%)
  matrix products  20.1 us (10%)
  between operations  14 us (7%)
  other arithmetic  4.13 us (2%)
  local copies, waits for them, and re-layouts  3.55 us (2%)
    ppermute x15, starting transfers between devices, pairwise_exchange(): lax.ppermute(sent, axis, [(i, i ^ step) for i in range(count)])  22.8 us
    all_to_all x1, waiting for transfers between devices, shards(): lax.all_to_all(turned, 'ctx', split_axis=2, concat_axis=1, tiled=True)  22.8 us
    all_to_all x1, waiting for transfers between devices, shards(): lax.all_to_all(first_section(sent_filter), 'ctx', split_axis=1, concat_ax...  21.2 us
    all_to_all x1, waiting for transfers between devices, shards(): lax.all_to_all(first_section(sent_input), 'ctx', split_axis=1, concat_axi...  20.3 us
    reduce_scatter x1, waiting for transfers between devices, shards(): lax.psum_scatter(lax.dot_general(w_out, gated, (((0,), (1,)), ((), ())),...  18.9 us
    dot_general x12, matrix products, cycle_apply(): return jnp.einsum('kn,zmnc->zmkc', table, operand, precision=precise)  12.8 us
    all_to_all x1, waiting for transfers between devices, shards(): lax.all_to_all(gated_in.reshape(1, ctx_size, per_dev, chan_width), 'ctx',...  7.8 us
    all_to_all x1, starting transfers between devices, shards(): lax.all_to_all(gated_in.reshape(1, ctx_size, per_dev, chan_width), 'ctx',...  7.36 us
  transfers between devices with their start and end apart: 21, of which 8 were waited for; matrix products, arithmetic and copies ran while one was open for 3% of the time, Pallas kernels for 0%

profile of v1, /device:TPU:0, one launch (start us, length us, event | category | flops | bytes accessed | tf_op | source)
XLA Modules:
  0.0 195.9 jit_solution(12934322489396149881)
XLA Ops:
  6.5 1.7 fusion.48
  8.2 7.4 %all-to-all-start = ((bf16[1,16,8,512]{3,2,0,1:T(8,128)(2,1)}), bf16[1,16,8,512]{3,2,0,1:T(8,128)(2,1)S(1)}, u32[]{:S(2)}, u32[]{:S(2)}) async-start(bf16[1,16,8,512]{3,2,0,1:T(8,128)(2,1)} %fusion.48), calls=%async_computation | async-start | bytes 262144 | tf_op jit(solution)/shard_map/all_to_all | solution.py:54
  15.7 7.8 %all-to-all-done = bf16[1,16,8,512]{3,2,0,1:T(8,128)(2,1)S(1)} async-done(((bf16[1,16,8,512]{3,2,0,1:T(8,128)(2,1)}), bf16[1,16,8,512]{3,2,0,1:T(8,128)(2,1)S(1)}, u32[]{:S(2)}, u32[]{:S(2)}) %all-to-all-start) | async-done | bytes 131104 | tf_op jit(solution)/shard_map/all_to_all | solution.py:54
  23.5 3.5 %all-to-all-start.2 = ((bf16[1,16,8,512]{3,2,0,1:T(8,128)(2,1)}), bf16[1,16,8,512]{3,2,0,1:T(8,128)(2,1)S(1)}, u32[]{:S(2)}, u32[]{:S(2)}) async-start(bf16[1,16,8,512]{3,2,0,1:T(8,128)(2,1)} %bitcast.245), calls=%async_computation.2 | async-start | bytes 262144 | tf_op jit(solution)/shard_map/all_to_all | solution.py:61
  27.0 0.5 convolution_negate_fusion.1
  27.5 0.5 fusion.23
  28.0 6.9 %all-to-all-done.2 = bf16[1,16,8,512]{3,2,0,1:T(8,128)(2,1)S(1)} async-done(((bf16[1,16,8,512]{3,2,0,1:T(8,128)(2,1)}), bf16[1,16,8,512]{3,2,0,1:T(8,128)(2,1)S(1)}, u32[]{:S(2)}, u32[]{:S(2)}) %all-to-all-start.2) | async-done | bytes 131104 | tf_op jit(solution)/shard_map/all_to_all | solution.py:61
  34.9 0.5 fusion.20
  35.4 0.6 multiply_add_fusion.1
  36.7 1.1 pad_maximum_fusion.1
  37.8 3.7 %all-to-all-start.3 = ((f32[2,16,2,8,512]{4,3,2,0,1:T(8,128)}), f32[2,16,2,8,512]{4,3,2,0,1:T(8,128)S(1)}, u32[]{:S(2)}, u32[]{:S(2)}) async-start(f32[2,16,2,8,512]{4,3,2,0,1:T(8,128)} %pad_maximum_fusion.1), calls=%async_computation.3 | async-start | bytes 2097152 | tf_op jit(solution)/shard_map/all_to_all | solution.py:92
  42.0 1.1 pad_maximum_fusion
  43.1 21.2 %all-to-all-done.3 = f32[2,16,2,8,512]{4,3,2,0,1:T(8,128)S(1)} async-done(((f32[2,16,2,8,512]{4,3,2,0,1:T(8,128)}), f32[2,16,2,8,512]{4,3,2,0,1:T(8,128)S(1)}, u32[]{:S(2)}, u32[]{:S(2)}) %all-to-all-start.3) | async-done | bytes 1048608 | tf_op jit(solution)/shard_map/all_to_all | solution.py:92
  64.3 7.0 %all-to-all-start.1 = ((f32[2,16,2,8,512]{4,3,2,0,1:T(8,128)}), f32[2,16,2,8,512]{4,3,2,0,1:T(8,128)S(1)}, u32[]{:S(2)}, u32[]{:S(2)}) async-start(f32[2,16,2,8,512]{4,3,2,0,1:T(8,128)} %pad_maximum_fusion), calls=%async_computation.1 | async-start | bytes 2097152 | tf_op jit(solution)/shard_map/all_to_all | solution.py:89
  71.5 1.1 fusion.15
  72.7 1.1 fusion.14
  73.8 20.3 %all-to-all-done.1 = f32[2,16,2,8,512]{4,3,2,0,1:T(8,128)S(1)} async-done(((f32[2,16,2,8,512]{4,3,2,0,1:T(8,128)}), f32[2,16,2,8,512]{4,3,2,0,1:T(8,128)S(1)}, u32[]{:S(2)}, u32[]{:S(2)}) %all-to-all-start.1) | async-done | bytes 1048608 | tf_op jit(solution)/shard_map/all_to_all | solution.py:89
  94.2 1.1 fusion.13
  95.3 1.1 fusion.12
  96.4 1.1 convolution_subtract_fusion.1
  97.5 1.1 convolution_add_fusion.1
  98.7 1.1 convolution_add_fusion.2
  99.8 1.1 multiply_subtract_fusion
  100.9 0.9 fusion.7
  101.8 0.9 fusion.9
  102.7 0.9 fusion.1
  103.6 1.2 subtract_bitcast_fusion
  104.9 1.1 copy.79
  106.0 7.0 %all-to-all-start.4 = ((f32[2,2,16,8,512]{4,3,1,0,2:T(8,128)}), f32[2,2,16,8,512]{4,3,1,0,2:T(8,128)S(1)}, u32[]{:S(2)}, u32[]{:S(2)}) async-start(f32[2,2,16,8,512]{4,3,1,0,2:T(8,128)} %copy.79), calls=%async_computation.4 | async-start | bytes 2097152 | tf_op jit(solution)/shard_map/all_to_all | solution.py:125
  113.2 22.8 %all-to-all-done.4 = f32[2,2,16,8,512]{4,3,1,0,2:T(8,128)S(1)} async-done(((f32[2,2,16,8,512]{4,3,1,0,2:T(8,128)}), f32[2,2,16,8,512]{4,3,1,0,2:T(8,128)S(1)}, u32[]{:S(2)}, u32[]{:S(2)}) %all-to-all-start.4) | async-done | bytes 1048608 | tf_op jit(solution)/shard_map/all_to_all | solution.py:125
  136.0 0.7 fusion.4
  136.7 0.7 convolution_subtract_fusion.3
  137.8 0.7 collective-permute-start
  138.5 2.0 %collective-permute-start.1 = (f32[1,1,8,512]{3,2,1,0:T(8,128)S(1)}, f32[1,1,8,512]{3,2,1,0:T(8,128)S(1)}, u32[]{:S(2)}, u32[]{:S(2)}) collective-permute-start(f32[1,1,8,512]{3,2,1,0:T(8,128)S(1)} %bitcast.258), channel_id=1, source_target_pairs={{0,4},{2,6},{4,0},{6,2},{8,12},{10,14},{12,8},{14,10},{16,20},{18,... | collective-permute-start | bytes 49160 | tf_op jit(solution)/shard_map/ppermute | solution.py:28
  140.4 2.9 %collective-permute-start.3 = (f32[1,1,8,512]{3,2,1,0:T(8,128)S(1)}, f32[1,1,8,512]{3,2,1,0:T(8,128)S(1)}, u32[]{:S(2)}, u32[]{:S(2)}) collective-permute-start(f32[1,1,8,512]{3,2,1,0:T(8,128)S(1)} %bitcast.254), channel_id=1, source_target_pairs={{0,8},{2,10},{4,12},{6,14},{8,0},{10,2},{12,4},{14,6},{16,24},{18,... | collective-permute-start | bytes 49160 | tf_op jit(solution)/shard_map/ppermute | solution.py:28
  143.7 2.7 %collective-permute-start.5 = (f32[1,1,8,512]{3,2,1,0:T(8,128)S(1)}, f32[1,1,8,512]{3,2,1,0:T(8,128)S(1)}, u32[]{:S(2)}, u32[]{:S(2)}) collective-permute-start(f32[1,1,8,512]{3,2,1,0:T(8,128)S(1)} %bitcast.259), channel_id=1, source_target_pairs={{0,12},{2,14},{4,8},{6,10},{8,4},{10,6},{12,0},{14,2},{16,28},{18,... | collective-permute-start | bytes 49160 | tf_op jit(solution)/shard_map/ppermute | solution.py:28
  146.5 2.9 %collective-permute-start.7 = (f32[1,1,8,512]{3,2,1,0:T(8,128)S(1)}, f32[1,1,8,512]{3,2,1,0:T(8,128)S(1)}, u32[]{:S(2)}, u32[]{:S(2)}) collective-permute-start(f32[1,1,8,512]{3,2,1,0:T(8,128)S(1)} %bitcast.255), channel_id=1, source_target_pairs={{0,16},{2,18},{4,20},{6,22},{8,24},{10,26},{12,28},{14,30},{16,0},... | collective-permute-start | bytes 49160 | tf_op jit(solution)/shard_map/ppermute | solution.py:28
  149.4 2.1 %collective-permute-start.9 = (f32[1,1,8,512]{3,2,1,0:T(8,128)S(1)}, f32[1,1,8,512]{3,2,1,0:T(8,128)S(1)}, u32[]{:S(2)}, u32[]{:S(2)}) collective-permute-start(f32[1,1,8,512]{3,2,1,0:T(8,128)S(1)} %bitcast.251), channel_id=1, source_target_pairs={{0,20},{2,22},{4,16},{6,18},{8,28},{10,30},{12,24},{14,26},{16,4},... | collective-permute-start | bytes 49160 | tf_op jit(solution)/shard_map/ppermute | solution.py:28
  151.5 1.2 collective-permute-start.10
  152.8 2.3 %collective-permute-start.11 = (f32[1,1,8,512]{3,2,1,0:T(8,128)S(1)}, f32[1,1,8,512]{3,2,1,0:T(8,128)S(1)}, u32[]{:S(2)}, u32[]{:S(2)}) collective-permute-start(f32[1,1,8,512]{3,2,1,0:T(8,128)S(1)} %bitcast.249), channel_id=1, source_target_pairs={{0,24},{2,26},{4,28},{6,30},{8,16},{10,18},{12,20},{14,22},{16,8},... | collective-permute-start | bytes 49160 | tf_op jit(solution)/shard_map/ppermute | solution.py:28
  155.1 1.5 collective-permute-start.12
  156.6 3.1 %collective-permute-start.13 = (f32[1,1,8,512]{3,2,1,0:T(8,128)S(1)}, f32[1,1,8,512]{3,2,1,0:T(8,128)S(1)}, u32[]{:S(2)}, u32[]{:S(2)}) collective-permute-start(f32[1,1,8,512]{3,2,1,0:T(8,128)S(1)} %bitcast.247), channel_id=1, source_target_pairs={{0,28},{2,30},{4,24},{6,26},{8,20},{10,22},{12,16},{14,18},{16,12}... | collective-permute-start | bytes 49160 | tf_op jit(solution)/shard_map/ppermute | solution.py:28
  159.7 1.0 collective-permute-start.14
  160.8 2.2 %collective-permute-done.13 = f32[1,1,8,512]{3,2,1,0:T(8,128)S(1)} collective-permute-done((f32[1,1,8,512]{3,2,1,0:T(8,128)S(1)}, f32[1,1,8,512]{3,2,1,0:T(8,128)S(1)}, u32[]{:S(2)}, u32[]{:S(2)}) %collective-permute-start.13) | collective-permute-done | bytes 16416 | tf_op jit(solution)/shard_map/ppermute | solution.py:28
  163.1 2.6 %collective-permute-done.14 = f32[1,1,8,512]{3,2,1,0:T(8,128)S(1)} collective-permute-done((f32[1,1,8,512]{3,2,1,0:T(8,128)S(1)}, f32[1,1,8,512]{3,2,1,0:T(8,128)S(1)}, u32[]{:S(2)}, u32[]{:S(2)}) %collective-permute-start.14) | collective-permute-done | bytes 16416 | tf_op jit(solution)/shard_map/ppermute | solution.py:28
  165.7 0.6 gather_fusion
  166.3 3.9 %fusion = bf16[4096,128]{0,1:T(8,128)(2,1)} fusion(bf16[512,4096]{1,0:T(8,128)(2,1)} %param.11, f32[16,8,512]{2,1,0:T(8,128)S(1)} %gather_fusion, bf16[128,512]{1,0:T(8,128)(2,1)S(1)} %copy-done.2, f32[512]{0:T(512)S(1)} %copy-done.3, bf16[128,512]{1,0:T(8,128)(2,1)S(1)} %copy-done, bf16[128,512]{1,0:T(8,128)(2,1)S(1)} %copy-done.1), kind=kOutput, calls=%fused_computation.2 | convolution fusion | flops 538050560 | bytes 5900288 | tf_op jit(solution)/shard_map/dot_general | solution.py:133
  170.2 18.9 %reduce-scatter.2.cloned.1.call-done = bf16[2048,128]{0,1:T(8,128)(2,1)} async-done(((bf16[4096,128]{0,1:T(8,128)(2,1)}), bf16[2048,128]{0,1:T(8,128)(2,1)}) %reduce-scatter.2.cloned.1.call-update) | async-done | bytes 524304 | tf_op jit(solution)/shard_map/reduce_scatter | solution.py:132
  (73 shorter events, 2.6 us)
Async XLA Ops:
  8.2 15.3 %all-to-all-start = ((bf16[1,16,8,512]{3,2,0,1:T(8,128)(2,1)}), bf16[1,16,8,512]{3,2,0,1:T(8,128)(2,1)S(1)}, u32[]{:S(2)}, u32[]{:S(2)}) async-start(bf16[1,16,8,512]{3,2,0,1:T(8,128)(2,1)} %fusion.48), calls=%async_computation | async-start | bytes 262144 | tf_op jit(solution)/shard_map/all_to_all | solution.py:54
  23.5 11.4 %all-to-all-start.2 = ((bf16[1,16,8,512]{3,2,0,1:T(8,128)(2,1)}), bf16[1,16,8,512]{3,2,0,1:T(8,128)(2,1)S(1)}, u32[]{:S(2)}, u32[]{:S(2)}) async-start(bf16[1,16,8,512]{3,2,0,1:T(8,128)(2,1)} %bitcast.245), calls=%async_computation.2 | async-start | bytes 262144 | tf_op jit(solution)/shard_map/all_to_all | solution.py:61
  37.8 26.6 %all-to-all-start.3 = ((f32[2,16,2,8,512]{4,3,2,0,1:T(8,128)}), f32[2,16,2,8,512]{4,3,2,0,1:T(8,128)S(1)}, u32[]{:S(2)}, u32[]{:S(2)}) async-start(f32[2,16,2,8,512]{4,3,2,0,1:T(8,128)} %pad_maximum_fusion.1), calls=%async_computation.3 | async-start | bytes 2097152 | tf_op jit(solution)/shard_map/all_to_all | solution.py:92
  64.3 29.8 %all-to-all-start.1 = ((f32[2,16,2,8,512]{4,3,2,0,1:T(8,128)}), f32[2,16,2,8,512]{4,3,2,0,1:T(8,128)S(1)}, u32[]{:S(2)}, u32[]{:S(2)}) async-start(f32[2,16,2,8,512]{4,3,2,0,1:T(8,128)} %pad_maximum_fusion), calls=%async_computation.1 | async-start | bytes 2097152 | tf_op jit(solution)/shard_map/all_to_all | solution.py:89
  106.0 60.2 %copy-start = (bf16[128,512]{1,0:T(8,128)(2,1)S(1)}, bf16[128,512]{1,0:T(8,128)(2,1)}, u32[]{:S(2)}) copy-start(bf16[128,512]{1,0:T(8,128)(2,1)} %param.8) | copy-start | bytes 393220
  106.0 60.3 %copy-start.1 = (bf16[128,512]{1,0:T(8,128)(2,1)S(1)}, bf16[128,512]{1,0:T(8,128)(2,1)}, u32[]{:S(2)}) copy-start(bf16[128,512]{1,0:T(8,128)(2,1)} %param.7) | copy-start | bytes 393220
  106.0 60.3 %copy-start.2 = (bf16[128,512]{1,0:T(8,128)(2,1)S(1)}, bf16[128,512]{1,0:T(8,128)(2,1)}, u32[]{:S(2)}) copy-start(bf16[128,512]{1,0:T(8,128)(2,1)} %param.6) | copy-start | bytes 393220
  106.0 60.3 %copy-start.3 = (f32[512]{0:T(512)S(1)}, f32[512]{0:T(512)}, u32[]{:S(2)}) copy-start(f32[512]{0:T(512)} %param.10) | copy-start | bytes 6148
  106.0 30.0 %all-to-all-start.4 = ((f32[2,2,16,8,512]{4,3,1,0,2:T(8,128)}), f32[2,2,16,8,512]{4,3,1,0,2:T(8,128)S(1)}, u32[]{:S(2)}, u32[]{:S(2)}) async-start(f32[2,2,16,8,512]{4,3,1,0,2:T(8,128)} %copy.79), calls=%async_computation.4 | async-start | bytes 2097152 | tf_op jit(solution)/shard_map/all_to_all | solution.py:125
  113.0 76.1 %reduce-scatter.2.cloned.1.call-start = ((), (), s32[]{:S(2)}) async-start(), calls=%async_computation.6 | async-start | bytes 1572864 | tf_op jit(solution)/shard_map/reduce_scatter | solution.py:132
  137.8 5.9 %collective-permute-start = (f32[1,1,8,512]{3,2,1,0:T(8,128)S(1)}, f32[1,1,8,512]{3,2,1,0:T(8,128)S(1)}, u32[]{:S(2)}, u32[]{:S(2)}) collective-permute-start(f32[1,1,8,512]{3,2,1,0:T(8,128)S(1)} %bitcast.260), channel_id=1, source_target_pairs={{0,2},{2,0},{4,6},{6,4},{8,10},{10,8},{12,14},{14,12},{16,18},{18,... | collective-permute-start | bytes 49160 | tf_op jit(solution)/shard_map/ppermute | solution.py:28
  138.5 8.0 %collective-permute-start.1 = (f32[1,1,8,512]{3,2,1,0:T(8,128)S(1)}, f32[1,1,8,512]{3,2,1,0:T(8,128)S(1)}, u32[]{:S(2)}, u32[]{:S(2)}) collective-permute-start(f32[1,1,8,512]{3,2,1,0:T(8,128)S(1)} %bitcast.258), channel_id=1, source_target_pairs={{0,4},{2,6},{4,0},{6,2},{8,12},{10,14},{12,8},{14,10},{16,20},{18,... | collective-permute-start | bytes 49160 | tf_op jit(solution)/shard_map/ppermute | solution.py:28
  140.4 6.0 %collective-permute-start.2 = (f32[1,1,8,512]{3,2,1,0:T(8,128)S(1)}, f32[1,1,8,512]{3,2,1,0:T(8,128)S(1)}, u32[]{:S(2)}, u32[]{:S(2)}) collective-permute-start(f32[1,1,8,512]{3,2,1,0:T(8,128)S(1)} %bitcast.256), channel_id=1, source_target_pairs={{0,6},{2,4},{4,2},{6,0},{8,14},{10,12},{12,10},{14,8},{16,22},{18,... | collective-permute-start | bytes 49160 | tf_op jit(solution)/shard_map/ppermute | solution.py:28
  140.4 9.0 %collective-permute-start.3 = (f32[1,1,8,512]{3,2,1,0:T(8,128)S(1)}, f32[1,1,8,512]{3,2,1,0:T(8,128)S(1)}, u32[]{:S(2)}, u32[]{:S(2)}) collective-permute-start(f32[1,1,8,512]{3,2,1,0:T(8,128)S(1)} %bitcast.254), channel_id=1, source_target_pairs={{0,8},{2,10},{4,12},{6,14},{8,0},{10,2},{12,4},{14,6},{16,24},{18,... | collective-permute-start | bytes 49160 | tf_op jit(solution)/shard_map/ppermute | solution.py:28
  143.3 6.1 %collective-permute-start.4 = (f32[1,1,8,512]{3,2,1,0:T(8,128)S(1)}, f32[1,1,8,512]{3,2,1,0:T(8,128)S(1)}, u32[]{:S(2)}, u32[]{:S(2)}) collective-permute-start(f32[1,1,8,512]{3,2,1,0:T(8,128)S(1)} %bitcast.252), channel_id=1, source_target_pairs={{0,10},{2,8},{4,14},{6,12},{8,2},{10,0},{12,6},{14,4},{16,26},{18,... | collective-permute-start | bytes 49160 | tf_op jit(solution)/shard_map/ppermute | solution.py:28
  143.7 7.8 %collective-permute-start.5 = (f32[1,1,8,512]{3,2,1,0:T(8,128)S(1)}, f32[1,1,8,512]{3,2,1,0:T(8,128)S(1)}, u32[]{:S(2)}, u32[]{:S(2)}) collective-permute-start(f32[1,1,8,512]{3,2,1,0:T(8,128)S(1)} %bitcast.259), channel_id=1, source_target_pairs={{0,12},{2,14},{4,8},{6,10},{8,4},{10,6},{12,0},{14,2},{16,28},{18,... | collective-permute-start | bytes 49160 | tf_op jit(solution)/shard_map/ppermute | solution.py:28
  146.4 6.3 %collective-permute-start.6 = (f32[1,1,8,512]{3,2,1,0:T(8,128)S(1)}, f32[1,1,8,512]{3,2,1,0:T(8,128)S(1)}, u32[]{:S(2)}, u32[]{:S(2)}) collective-permute-start(f32[1,1,8,512]{3,2,1,0:T(8,128)S(1)} %bitcast.257), channel_id=1, source_target_pairs={{0,14},{2,12},{4,10},{6,8},{8,6},{10,4},{12,2},{14,0},{16,30},{18,... | collective-permute-start | bytes 49160 | tf_op jit(solution)/shard_map/ppermute | solution.py:28
  146.5 8.6 %collective-permute-start.7 = (f32[1,1,8,512]{3,2,1,0:T(8,128)S(1)}, f32[1,1,8,512]{3,2,1,0:T(8,128)S(1)}, u32[]{:S(2)}, u32[]{:S(2)}) collective-permute-start(f32[1,1,8,512]{3,2,1,0:T(8,128)S(1)} %bitcast.255), channel_id=1, source_target_pairs={{0,16},{2,18},{4,20},{6,22},{8,24},{10,26},{12,28},{14,30},{16,0},... | collective-permute-start | bytes 49160 | tf_op jit(solution)/shard_map/ppermute | solution.py:28
  149.4 7.2 %collective-permute-start.8 = (f32[1,1,8,512]{3,2,1,0:T(8,128)S(1)}, f32[1,1,8,512]{3,2,1,0:T(8,128)S(1)}, u32[]{:S(2)}, u32[]{:S(2)}) collective-permute-start(f32[1,1,8,512]{3,2,1,0:T(8,128)S(1)} %bitcast.253), channel_id=1, source_target_pairs={{0,18},{2,16},{4,22},{6,20},{8,26},{10,24},{12,30},{14,28},{16,2},... | collective-permute-start | bytes 49160 | tf_op jit(solution)/shard_map/ppermute | solution.py:28
  149.4 10.3 %collective-permute-start.9 = (f32[1,1,8,512]{3,2,1,0:T(8,128)S(1)}, f32[1,1,8,512]{3,2,1,0:T(8,128)S(1)}, u32[]{:S(2)}, u32[]{:S(2)}) collective-permute-start(f32[1,1,8,512]{3,2,1,0:T(8,128)S(1)} %bitcast.251), channel_id=1, source_target_pairs={{0,20},{2,22},{4,16},{6,18},{8,28},{10,30},{12,24},{14,26},{16,4},... | collective-permute-start | bytes 49160 | tf_op jit(solution)/shard_map/ppermute | solution.py:28
  151.5 9.2 %collective-permute-start.10 = (f32[1,1,8,512]{3,2,1,0:T(8,128)S(1)}, f32[1,1,8,512]{3,2,1,0:T(8,128)S(1)}, u32[]{:S(2)}, u32[]{:S(2)}) collective-permute-start(f32[1,1,8,512]{3,2,1,0:T(8,128)S(1)} %bitcast.250), channel_id=1, source_target_pairs={{0,22},{2,20},{4,18},{6,16},{8,30},{10,28},{12,26},{14,24},{16,6},... | collective-permute-start | bytes 49160 | tf_op jit(solution)/shard_map/ppermute | solution.py:28
  152.8 8.0 %collective-permute-start.11 = (f32[1,1,8,512]{3,2,1,0:T(8,128)S(1)}, f32[1,1,8,512]{3,2,1,0:T(8,128)S(1)}, u32[]{:S(2)}, u32[]{:S(2)}) collective-permute-start(f32[1,1,8,512]{3,2,1,0:T(8,128)S(1)} %bitcast.249), channel_id=1, source_target_pairs={{0,24},{2,26},{4,28},{6,30},{8,16},{10,18},{12,20},{14,22},{16,8},... | collective-permute-start | bytes 49160 | tf_op jit(solution)/shard_map/ppermute | solution.py:28
  155.1 5.7 %collective-permute-start.12 = (f32[1,1,8,512]{3,2,1,0:T(8,128)S(1)}, f32[1,1,8,512]{3,2,1,0:T(8,128)S(1)}, u32[]{:S(2)}, u32[]{:S(2)}) collective-permute-start(f32[1,1,8,512]{3,2,1,0:T(8,128)S(1)} %bitcast.248), channel_id=1, source_target_pairs={{0,26},{2,24},{4,30},{6,28},{8,18},{10,16},{12,22},{14,20},{16,10}... | collective-permute-start | bytes 49160 | tf_op jit(solution)/shard_map/ppermute | solution.py:28
  156.6 6.4 %collective-permute-start.13 = (f32[1,1,8,512]{3,2,1,0:T(8,128)S(1)}, f32[1,1,8,512]{3,2,1,0:T(8,128)S(1)}, u32[]{:S(2)}, u32[]{:S(2)}) collective-permute-start(f32[1,1,8,512]{3,2,1,0:T(8,128)S(1)} %bitcast.247), channel_id=1, source_target_pairs={{0,28},{2,30},{4,24},{6,26},{8,20},{10,22},{12,16},{14,18},{16,12}... | collective-permute-start | bytes 49160 | tf_op jit(solution)/shard_map/ppermute | solution.py:28
  159.7 5.9 %collective-permute-start.14 = (f32[1,1,8,512]{3,2,1,0:T(8,128)S(1)}, f32[1,1,8,512]{3,2,1,0:T(8,128)S(1)}, u32[]{:S(2)}, u32[]{:S(2)}) collective-permute-start(f32[1,1,8,512]{3,2,1,0:T(8,128)S(1)} %bitcast.246), channel_id=1, source_target_pairs={{0,30},{2,28},{4,26},{6,24},{8,22},{10,20},{12,18},{14,16},{16,14}... | collective-permute-start | bytes 49160 | tf_op jit(solution)/shard_map/ppermute | solution.py:28
Sparse Core Ops, SparseCore 0:
  170.3 18.7 reduce-scatter.1
